TPU v7x, 32 devices: a whole 2x2x4 slice. The times are simulated.
32 devices in a mesh: passage: 4 (over z), cell: 4 (over y, x), tm: 2 (over core).
Axes of the slice: x: 2, y: 2, z: 4, core: 2. Of those that a mesh axis runs over, the one named last changes fastest.
Arguments:
- adjoint_start: float32 [8, 5, 8, 1024, 256], P('tm', None, 'cell', 'passage'), may hold values from -6 to 6
- adjoint_source: float32 [8, 5, 8, 1024, 256], P('tm', None, 'cell', 'passage'), may hold values from -6 to 6
- jacobian: bfloat16 [2, 5, 5, 8, 1024, 256], P(None, None, None, 'cell', 'passage'), may hold values from -2.5 to 2.5
- pseudo_time: float32 [8, 1024, 256], P('cell', 'passage'), may hold values from 3 to 12
- dissipation: float32 [8, 1024, 256], P('cell', 'passage'), may hold values from 0.2 to 1
- surface_cells: int32 [4, 1024], P('cell'), may hold values from 0 to 1023, as said below
- surface_weights: float32 [8, 5, 4096], P('tm', None, 'cell'), may hold values from -1 to 1
Outputs:
- adjoint_final: float32 [8, 5, 8, 1024, 256], P('tm', None, 'cell', 'passage')
- diameter_modes: float32 [2, 16, 4096], P(None, None, 'cell')
Inputs may be any that keep to these rules, and one draw needn't show every extreme that they name: `surface_cells`: each row holds every value from 0 to 1023 exactly once, in a drawn order.
All inputs are finite; a program needn't handle non-finite values.
Results may differ from a plain program's by a relative error of at most 0.0025.
Values may be sent and summed in bfloat16 or wider, within the bound.
A program may use at most 256 MiB of HBM per device.

v0:
```python
import jax
import jax.numpy as jnp
from jax import lax
from jax.sharding import PartitionSpec as P

PASSAGES = 16
CJ = 64
SWEEPS = 2
OMEGA = 1.0


def with_halo(array, sides, width, wrap):
    for axis, dim in sides:
        peers, length = (lax.axis_size(axis), array.shape[dim])
        up = [(i, (i + 1) % peers) for i in range(peers if wrap else peers - 1)]
        down = [(j, i) for i, j in up]
        last = lax.slice_in_dim(array, length - width, length, axis=dim)
        leading = lax.slice_in_dim(array, 0, width, axis=dim)
        before = lax.ppermute(last, axis, up)
        after = lax.ppermute(leading, axis, down)
        array = jnp.concatenate([before, array, after], axis=dim)
    return array


def spectral_matrix(total):
    index = jnp.arange(total, dtype=jnp.int32)
    offset = index[:, None] - index[None, :]
    parity = (1 - 2 * (offset % 2)).astype(jnp.float32)
    phase_arg = jnp.pi * offset.astype(jnp.float32) / total
    sine_safe = jnp.where(offset == 0, jnp.float32(1.0), jnp.sin(phase_arg))
    values = 0.5 * parity * jnp.cos(phase_arg) / sine_safe
    return jnp.where(offset == 0, jnp.float32(0.0), values)


def blade_table(passages):
    index = jnp.arange(passages, dtype=jnp.int32)
    product_mod = index[:, None] * index[None, :] % passages
    phase_arg = 2.0 * jnp.pi * product_mod.astype(jnp.float32) / passages
    factor = 1.0 / passages**0.5
    return jnp.stack([jnp.cos(phase_arg), -jnp.sin(phase_arg)]) * factor


def adjoint_operator(field, plus_i, minus_i, plus_j, minus_j, jacobian, sigma, damping):
    total_out = sigma * field + damping * (4.0 * field - plus_i - minus_i - plus_j - minus_j)
    variables = field.shape[1]
    flux_rows = []
    for target_var in range(variables):
        acc_flux = jnp.zeros_like(field[:, 0])
        for source_var in range(variables):
            acc_flux = acc_flux + jacobian[0, source_var, target_var].astype(jnp.float32) * (
                field[:, source_var] - plus_i[:, source_var]
            )
            acc_flux = acc_flux + jacobian[1, source_var, target_var].astype(jnp.float32) * (
                field[:, source_var] - plus_j[:, source_var]
            )
        flux_rows.append(acc_flux)
    return total_out + jnp.stack(flux_rows, axis=1)


def neighbours(field):
    wrapped_field = with_halo(field, (("passage", 3),), 1, True)
    plus_j = wrapped_field[:, :, :, 2:]
    minus_j = wrapped_field[:, :, :, :-2]
    opened_field = with_halo(field.astype(jnp.bfloat16), (("cell", 2),), 1, False).astype(
        field.dtype
    )
    plus_i = opened_field[:, :, 2:]
    minus_i = opened_field[:, :, :-2]
    return (plus_i, minus_i, plus_j, minus_j)


def body(
    adjoint_start,
    adjoint_source,
    jacobian,
    pseudo_time,
    dissipation,
    surface_cells,
    surface_weights,
):
    local_times = adjoint_start.shape[0]
    all_times = local_times * lax.axis_size("tm")
    dmatrix = spectral_matrix(all_times)
    first_time = lax.axis_index("tm") * local_times
    start_rounded = adjoint_start.astype(jnp.bfloat16)
    own_columns = lax.dynamic_slice_in_dim(dmatrix, first_time, local_times, 1)
    spectral_term = OMEGA * jnp.einsum(
        "ab,avipk->bvipk",
        own_columns,
        lax.all_gather(start_rounded, "tm", axis=0, tiled=True).astype(jnp.float32),
        precision=lax.Precision.HIGHEST,
    )
    scaling = 1.0 / (pseudo_time + 4.0 * dissipation)
    field = adjoint_start
    for sweep_index in range(SWEEPS):
        plus_i, minus_i, plus_j, minus_j = neighbours(field)
        applied = adjoint_operator(
            field, plus_i, minus_i, plus_j, minus_j, jacobian, pseudo_time, dissipation
        )
        field = field + (adjoint_source - applied - spectral_term) * scaling
    variables = field.shape[1]
    stream_cells = field.shape[2]
    pitch_cells = field.shape[3]
    span_cells = field.shape[4]
    first_pitch = lax.axis_index("passage") * pitch_cells
    side_rows = (
        jnp.arange(PASSAGES, dtype=jnp.int32)[:, None] * CJ
        + jnp.arange(2, dtype=jnp.int32)[None, :] * (CJ - 1)
    ).reshape(2 * PASSAGES)
    local_rows = side_rows - first_pitch
    owned = (local_rows >= 0) & (local_rows < pitch_cells)
    clipped = jnp.clip(local_rows, 0, pitch_cells - 1)
    rows = jnp.take(field, clipped, axis=3)
    rows = jnp.where(owned[None, None, None, :, None], rows, jnp.float32(0.0))
    rows = rows.reshape(local_times, variables, stream_cells, PASSAGES, 2, span_cells)
    rows = rows.transpose(0, 1, 3, 4, 2, 5).reshape(
        local_times, variables, PASSAGES, 2 * stream_cells * span_cells
    )
    picked = jnp.take(rows, surface_cells[0], axis=3)
    partial_sens = jnp.einsum(
        "tvs,tvps->ps", surface_weights, picked, precision=lax.Precision.HIGHEST
    )
    table = blade_table(PASSAGES)
    mode_terms = jnp.einsum("cmp,ps->cms", table, partial_sens, precision=lax.Precision.HIGHEST)
    diameter_modes = lax.psum(mode_terms, ("passage", "tm"))
    return (field, diameter_modes)


def solution(mesh):
    in_specs = (
        P("tm", None, "cell", "passage", None),
        P("tm", None, "cell", "passage", None),
        P(None, None, None, "cell", "passage", None),
        P("cell", "passage", None),
        P("cell", "passage", None),
        P("cell", None),
        P("tm", None, "cell"),
    )
    out_specs = (P("tm", None, "cell", "passage", None), P(None, None, "cell"))
    return jax.shard_map(body, mesh=mesh, in_specs=in_specs, out_specs=out_specs, check_vma=False)
```

profile of v0, /device:TPU:0, one launch (start us, length us, event | category | flops | bytes accessed | tf_op | source)
XLA Modules:
  0.0 580.4 jit_solution(5656503605032928733)
XLA Ops:
  7.2 13.1 %copy.108 = bf16[4,5,2,256,256]{4,0,3,2,1:T(4,128)(2,1)} copy(f32[4,5,2,256,256]{4,3,2,1,0:T(8,128)} %param.7) | data formatting | bytes 15728640 | tf_op args[0]
  20.3 7.0 %fusion.71 = (bf16[4,5,1,256,256]{4,0,3,2,1:T(4,128)(2,1)}, bf16[4,5,1,256,256]{4,0,3,2,1:T(4,128)(2,1)}) fusion(bf16[4,5,2,256,256]{4,0,3,2,1:T(4,128)(2,1)} %copy.108), kind=kLoop, calls=%fused_computation.188 | loop fusion | bytes 10485760 | tf_op jit(solution)/shard_map/slice | solution.py:17
  27.4 5.0 collective-permute-start
  37.2 15.7 %constant_dynamic-update-slice_fusion.1 = (f32[4,5,2,257,256]{4,0,3,2,1:T(4,128)}, f32[4,5,2,256,256]{4,0,3,2,1:T(4,128)S(1)}) fusion(f32[4,5,2,256,256]{4,3,2,1,0:T(8,128)} %param.7), kind=kLoop, calls=%fused_computation.132 | loop fusion | bytes 31457280
  52.9 5.7 copy-done.7
  63.2 4.3 bitcast_convert_fusion
  71.4 3.9 bitcast_convert_fusion.9
  76.0 12.7 %collective-permute-done = bf16[4,5,1,256,256]{4,0,3,2,1:T(4,128)(2,1)S(1)} collective-permute-done((bf16[4,5,1,256,256]{4,0,3,2,1:T(4,128)(2,1)}, bf16[4,5,1,256,256]{4,0,3,2,1:T(4,128)(2,1)S(1)}, u32[]{:S(2)}, u32[]{:S(2)}) %collective-permute-start) | collective-permute-done | bytes 2621472 | tf_op jit(solution)/shard_map/ppermute | solution.py:19
  88.7 58.1 %collective-permute-done.1 = bf16[4,5,1,256,256]{4,0,3,2,1:T(4,128)(2,1)} collective-permute-done((bf16[4,5,1,256,256]{4,0,3,2,1:T(4,128)(2,1)}, bf16[4,5,1,256,256]{4,0,3,2,1:T(4,128)(2,1)}, u32[]{:S(2)}, u32[]{:S(2)}) %collective-permute-start.1) | collective-permute-done | bytes 2621472 | tf_op jit(solution)/shard_map/ppermute | solution.py:20
  146.8 13.4 %add_dynamic-update-slice_fusion.9 = (f32[4,5,2,256,256]{4,0,3,2,1:T(4,128)}, f32[4,1,2,256,256]{4,0,3,2,1:T(4,128)S(1)}, f32[4,1,2,256,256]{4,0,3,2,1:T(4,128)S...) fusion(f32[2,256,256]{2,1,0:T(8,128)} %get-tuple-element.76, ...), kind=kLoop, calls=%fused_computation.74 | loop fusion | flops 30932992 | bytes 59768832
  160.3 11.0 %add_dynamic-update-slice_fusion.8 = f32[4,5,2,256,256]{4,0,3,2,1:T(4,128)} fusion(f32[4,5,2,256,256]{4,0,3,2,1:T(4,128)} %get-tuple-element.25, f32[4,1,2,256,256]{4,0,3,2,1:T(4,128)} %get-tuple-element.35, f32[4,1,2,256,256]{4,0,3,2,1:T(4,128)S(1)} %get-tuple-element.34, f32[4,1,2,256,256]{4,0,3,2,1:T(4,128)S(1)} %get-tuple-element.33, ...), kind=kLoop, calls=%fused_computation.73 | loop fusion | flops 9961472 | bytes 28311552
  171.3 9.5 %add_dynamic-update-slice_fusion.7 = f32[4,5,2,256,256]{4,0,3,2,1:T(4,128)} fusion(f32[4,5,2,256,256]{4,0,3,2,1:T(4,128)} %add_dynamic-update-slice_fusion.8, f32[4,1,2,256,256]{4,0,3,2,1:T(4,128)} %get-tuple-element.35, f32[4,1,2,256,256]{4,0,3,2,1:T(4,128)S(1)} %get-tuple-element.34, f32[4,1,2,256,256]{4,0,3,2,1:T(4,128)S(1)} %get-tuple-element.33, ...), kind=kLoop, calls=%fused_computation.72 | loop fusion | flops 9961472 | bytes 28311552
  180.8 8.1 %add_dynamic-update-slice_fusion.6 = f32[4,5,2,256,256]{4,0,3,2,1:T(4,128)} fusion(f32[4,5,2,256,256]{4,0,3,2,1:T(4,128)} %add_dynamic-update-slice_fusion.7, f32[4,1,2,256,256]{4,0,3,2,1:T(4,128)} %get-tuple-element.35, f32[4,1,2,256,256]{4,0,3,2,1:T(4,128)} %copy-done.6, f32[4,1,2,256,256]{4,0,3,2,1:T(4,128)} %copy-done.5, ...), kind=kLoop, calls=%fused_computation.71 | loop fusion | flops 9961472 | bytes 28311552
  188.9 8.0 %add_dynamic-update-slice_fusion.5 = f32[4,5,2,256,256]{4,0,3,2,1:T(4,128)} fusion(f32[4,5,2,256,256]{4,0,3,2,1:T(4,128)} %add_dynamic-update-slice_fusion.6, f32[4,1,2,256,256]{4,0,3,2,1:T(4,128)} %get-tuple-element.35, f32[4,1,2,256,256]{4,0,3,2,1:T(4,128)} %copy-done.6, f32[4,1,2,256,256]{4,0,3,2,1:T(4,128)} %copy-done.5, ...), kind=kLoop, calls=%fused_computation.70 | loop fusion | flops 9961472 | bytes 28311552 | tf_op jit(solution)/shard_map/stack | solution.py:57
  197.0 13.2 %maximum_convert_fusion = f32[4,5,4,256,256]{4,0,3,2,1:T(4,128)} fusion(bf16[4,5,1,256,256]{4,0,3,2,1:T(4,128)(2,1)} %collective-permute-done.1, bf16[4,5,2,256,256]{4,0,3,2,1:T(4,128)(2,1)S(1)} %bitcast.179, bf16[4,5,1,256,256]{4,0,3,2,1:T(4,128)(2,1)} %copy-done.8), kind=kLoop, calls=%fused_computation.30 | loop fusion | flops 15728640 | bytes 31457280 | tf_op jit(solution)/shard_map/convert_element_type | solution.py:64
  210.2 44.5 %fusion.66 = (bf16[4,5,2,256,256]{4,0,3,2,1:T(4,128)(2,1)}, f32[4,5,2,256,256]{4,0,3,2,1:T(4,128)}, f32[4,5,2,256,256]{4,0,3,2,1:T(4,128)}) fusion(f32[4,5,2,256,256]{4,0,3,2,1:T(4,128)} %copy-done.7, f32[2,256,256]{2,1,0:T(8,128)S(1)} %copy-done.20, f32[4,5,2,256,256]{4,0,3,2,1:T(4,128)} %add_dynamic-update-slice_fusion.5, ...), kind=kOutput, calls=%fused_computation.184 | convolution fusion | flops 290979840 | bytes 101230592 | tf_op jit(solution)/shard_map/ab,avipk->bvipk/dot_general | solution.py:87
  254.8 7.0 %fusion.70 = (bf16[4,5,1,256,256]{4,0,3,2,1:T(4,128)(2,1)}, bf16[4,5,1,256,256]{4,0,3,2,1:T(4,128)(2,1)}) fusion(bf16[4,5,2,256,256]{4,0,3,2,1:T(4,128)(2,1)} %get-tuple-element.23), kind=kLoop, calls=%fused_computation.187 | loop fusion | bytes 10485760 | tf_op jit(solution)/shard_map/slice | solution.py:17
  278.4 42.3 %collective-permute-done.4 = bf16[4,5,1,256,256]{4,0,3,2,1:T(4,128)(2,1)S(1)} collective-permute-done((bf16[4,5,1,256,256]{4,0,3,2,1:T(4,128)(2,1)}, bf16[4,5,1,256,256]{4,0,3,2,1:T(4,128)(2,1)S(1)}, u32[]{:S(2)}, u32[]{:S(2)}) %collective-permute-start.4) | collective-permute-done | bytes 2621472 | tf_op jit(solution)/shard_map/ppermute | solution.py:19
  322.3 55.4 %collective-permute-done.5 = bf16[4,5,1,256,256]{4,0,3,2,1:T(4,128)(2,1)} collective-permute-done((bf16[4,5,1,256,256]{4,0,3,2,1:T(4,128)(2,1)}, bf16[4,5,1,256,256]{4,0,3,2,1:T(4,128)(2,1)}, u32[]{:S(2)}, u32[]{:S(2)}) %collective-permute-start.5) | collective-permute-done | bytes 2621472 | tf_op jit(solution)/shard_map/ppermute | solution.py:20
  377.7 18.1 %add_dynamic-update-slice_fusion.4 = (f32[4,5,2,256,256]{4,0,3,2,1:T(4,128)}, f32[4,1,2,256,256]{4,0,3,2,1:T(4,128)S(1)}, f32[4,1,2,256,256]{4,0,3,2,1:T(4,128)S...) fusion(f32[2,256,256]{2,1,0:T(8,128)} %get-tuple-element.76, ...), kind=kLoop, calls=%fused_computation.69 | loop fusion | flops 33554432 | bytes 59809792
  395.8 8.4 %add_dynamic-update-slice_fusion.3 = f32[4,5,2,256,256]{4,0,3,2,1:T(4,128)} fusion(f32[4,5,2,256,256]{4,0,3,2,1:T(4,128)} %get-tuple-element.12, f32[4,1,2,256,256]{4,0,3,2,1:T(4,128)S(1)} %get-tuple-element.22, f32[4,1,2,256,256]{4,0,3,2,1:T(4,128)S(1)} %get-tuple-element.21, f32[4,1,2,256,256]{4,0,3,2,1:T(4,128)S(1)} %get-tuple-element.20, ...), kind=kLoop, calls=%fused_computation.68 | loop fusion | flops 9961472 | bytes 28311552
  404.2 7.0 %add_dynamic-update-slice_fusion.2 = f32[4,5,2,256,256]{4,0,3,2,1:T(4,128)} fusion(f32[4,5,2,256,256]{4,0,3,2,1:T(4,128)} %add_dynamic-update-slice_fusion.3, f32[4,1,2,256,256]{4,0,3,2,1:T(4,128)S(1)} %get-tuple-element.22, f32[4,1,2,256,256]{4,0,3,2,1:T(4,128)S(1)} %get-tuple-element.21, f32[4,1,2,256,256]{4,0,3,2,1:T(4,128)S(1)} %get-tuple-element.20, ...), kind=kLoop, calls=%fused_computation.67 | loop fusion | flops 9961472 | bytes 28311552
  411.3 7.1 %add_dynamic-update-slice_fusion.1 = f32[4,5,2,256,256]{4,0,3,2,1:T(4,128)} fusion(f32[4,5,2,256,256]{4,0,3,2,1:T(4,128)} %add_dynamic-update-slice_fusion.2, f32[4,1,2,256,256]{4,0,3,2,1:T(4,128)S(1)} %get-tuple-element.22, f32[4,1,2,256,256]{4,0,3,2,1:T(4,128)S(1)} %get-tuple-element.21, f32[4,1,2,256,256]{4,0,3,2,1:T(4,128)S(1)} %get-tuple-element.20, ...), kind=kLoop, calls=%fused_computation.66 | loop fusion | flops 9961472 | bytes 28311552
  418.4 9.7 %add_dynamic-update-slice_fusion = f32[4,5,2,256,256]{4,0,3,2,1:T(4,128)} fusion(f32[4,5,2,256,256]{4,0,3,2,1:T(4,128)} %add_dynamic-update-slice_fusion.1, f32[4,1,2,256,256]{4,0,3,2,1:T(4,128)} %copy-done.4, f32[4,1,2,256,256]{4,0,3,2,1:T(4,128)} %copy-done.3, f32[4,1,2,256,256]{4,0,3,2,1:T(4,128)} %copy-done.2, f32[4,1,2,256,256]{4,0,3,2,1:T(4,128)} %copy-done.1, ...), kind=kLoop, calls=%fused_computation.65 | loop fusion | flops 9961472 | bytes 28311552 | tf_op jit(solution)/shard_map/stack | solution.py:57
  428.2 15.2 %maximum_convert_fusion.1 = f32[4,5,4,256,256]{4,0,3,2,1:T(4,128)} fusion(bf16[4,5,1,256,256]{4,0,3,2,1:T(4,128)(2,1)} %collective-permute-done.5, bf16[4,5,2,256,256]{4,0,3,2,1:T(4,128)(2,1)} %get-tuple-element.23, bf16[4,5,1,256,256]{4,0,3,2,1:T(4,128)(2,1)} %copy-done.9), kind=kLoop, calls=%fused_computation.31 | loop fusion | flops 15728640 | bytes 31457280 | tf_op jit(solution)/shard_map/convert_element_type | solution.py:64
  443.4 28.2 %multiply_add_fusion = f32[4,5,2,256,256]{4,0,3,2,1:T(4,128)} fusion(f32[4,5,2,256,256]{4,0,3,2,1:T(4,128)S(1)} %bitcast.181, f32[4,5,2,256,256]{4,0,3,2,1:T(4,128)} %get-tuple-element.97, f32[4,5,2,256,256]{4,0,3,2,1:T(4,128)} %add_dynamic-update-slice_fusion, f32[4,5,2,1,256]{4,0,3,2,1:T(4,128)} %collective-permute-done.7, ...), kind=kLoop, calls=%fused_computation.35 | loop fusion | flops 39321600 | bytes 75055104 | tf_op jit(solution)/shard_map/add | solution.py:100
  471.7 5.5 gather_fusion
  478.3 7.1 %copy.94 = f32[4,5,16,2,2,256]{2,0,5,4,3,1:T(4,128)} copy(f32[4,5,16,2,2,256]{5,4,3,2,1,0:T(2,128)S(1)} %fusion.28) | data formatting | bytes 2621440 | tf_op jit(solution)/shard_map/reshape | solution.py:116
  485.3 20.8 %gather_fusion.1 = f32[1024,4,5,16]{3,1,2,0:T(4,128)} fusion(f32[4,5,16,1024]{2,0,3,1:T(4,128)} %bitcast.182, s32[1024]{0:T(1024)S(1)} %copy-done.25), kind=kCustom, calls=%fused_computation.1 | custom fusion | bytes 2625536 | tf_op jit(solution)/shard_map/jit(_take)/gather | solution.py:119
  506.1 9.9 %multiply_reduce_fusion = f32[1024,16]{1,0:T(8,128)S(1)} fusion(f32[1024,4,5,16]{3,1,2,0:T(4,128)} %gather_fusion.1, f32[1024,4,5]{1,2,0:T(8,128)} %copy.96, pred[1024]{0:T(1024)(128)(4,1)S(1)} %copy-done.29), kind=kLoop, calls=%fused_computation.32 | loop fusion | flops 966656 | bytes 1459200
  517.3 10.1 %copy.85 = f32[4,5,2,256,256]{4,3,2,1,0:T(8,128)} copy(f32[4,5,2,256,256]{4,0,3,2,1:T(4,128)} %multiply_add_fusion) | data formatting | bytes 20971520
  527.4 44.4 %all-reduce.2.cloned.1.call-done = f32[2,16,1024]{2,1,0:T(8,128)} async-done(((f32[2,16,1024]{2,1,0:T(8,128)}), f32[2,16,1024]{2,1,0:T(8,128)}) %all-reduce.2.cloned.1.call-update) | async-done | bytes 131088 | tf_op jit(solution)/shard_map/psum | solution.py:125
  (120 shorter events, 36.1 us)
Async XLA Ops:
  7.2 203.1 %all-gather.2.cloned.1.call-start = ((), (), s32[]{:S(2)}) async-start(), calls=%async_computation | async-start | bytes 15728640 | tf_op jit(solution)/shard_map/all_gather | solution.py:90
  20.3 13.4 %copy-start = (bf16[4,5,2,256,256]{4,0,3,2,1:T(4,128)(2,1)S(1)}, bf16[4,5,2,256,256]{4,0,3,2,1:T(4,128)(2,1)}, u32[]{:S(2)}) copy-start(bf16[4,5,2,256,256]{4,0,3,2,1:T(4,128)(2,1)} %copy.108) | copy-start | bytes 15728644
  27.4 61.3 %collective-permute-start = (bf16[4,5,1,256,256]{4,0,3,2,1:T(4,128)(2,1)}, bf16[4,5,1,256,256]{4,0,3,2,1:T(4,128)(2,1)S(1)}, u32[]{:S(2)}, u32[]{:S(2)}) collective-permute-start(bf16[4,5,1,256,256]{4,0,3,2,1:T(4,128)(2,1)} %get-tuple-element.94), channel_id=1, source_target_pairs={{0,2},{2,4},{4,6},{1,3},{3,5},{5,7},{8,10},{10,12},{12,14},{9,11},... | collective-permute-start | bytes 7864328 | tf_op jit(solution)/shard_map/ppermute | solution.py:19
  32.4 114.4 %collective-permute-start.1 = (bf16[4,5,1,256,256]{4,0,3,2,1:T(4,128)(2,1)}, bf16[4,5,1,256,256]{4,0,3,2,1:T(4,128)(2,1)}, u32[]{:S(2)}, u32[]{:S(2)}) collective-permute-start(bf16[4,5,1,256,256]{4,0,3,2,1:T(4,128)(2,1)} %get-tuple-element.95), channel_id=1, source_target_pairs={{2,0},{4,2},{6,4},{3,1},{5,3},{7,5},{10,8},{12,10},{14,12},{11,9},... | collective-permute-start | bytes 7864328 | tf_op jit(solution)/shard_map/ppermute | solution.py:20
  37.0 25.3 %copy-start.14 = (f32[2,256,256]{2,1,0:T(8,128)S(1)}, f32[2,256,256]{2,1,0:T(8,128)}, u32[]{:S(2)}) copy-start(f32[2,256,256]{2,1,0:T(8,128)} %param.10) | copy-start | bytes 1572868
  37.0 534.8 %all-reduce.2.cloned.1.call-start = ((), (), s32[]{:S(2)}) async-start(), calls=%async_computation.1 | async-start | bytes 262144 | tf_op jit(solution)/shard_map/psum | solution.py:125
  37.2 25.1 %copy-start.17 = (f32[2,256,256]{2,1,0:T(8,128)S(1)}, f32[2,256,256]{2,1,0:T(8,128)}, u32[]{:S(2)}) copy-start(f32[2,256,256]{2,1,0:T(8,128)} %param.11) | copy-start | bytes 1572868
  37.2 30.3 %slice-start.5 = ((s8[13107200]{0:T(1024)(128)(4,1)}), s8[4194304]{0:T(1024)(128)(4,1)S(1)}, s32[]{:S(2)}) async-start(s8[13107200]{0:T(1024)(128)(4,1)} %bitcast.183), calls=%async_computation.7 | async-start | bytes 8388608
  37.2 30.3 %slice-start.6 = ((s8[13107200]{0:T(1024)(128)(4,1)}), s8[4194304]{0:T(1024)(128)(4,1)S(1)}, s32[]{:S(2)}) async-start(s8[13107200]{0:T(1024)(128)(4,1)} %bitcast.183), calls=%async_computation.8 | async-start | bytes 8388608
  37.2 30.3 %slice-start.7 = ((s8[13107200]{0:T(1024)(128)(4,1)}), s8[4194304]{0:T(1024)(128)(4,1)S(1)}, s32[]{:S(2)}) async-start(s8[13107200]{0:T(1024)(128)(4,1)} %bitcast.183), calls=%async_computation.9 | async-start | bytes 8388608
  58.6 16.7 %collective-permute-start.2 = (f32[4,5,2,1,256]{4,0,3,2,1:T(4,128)S(1)}, f32[4,5,2,1,256]{4,0,3,2,1:T(4,128)S(1)}, u32[]{:S(2)}, u32[]{:S(2)}) collective-permute-start(f32[4,5,2,1,256]{4,0,3,2,1:T(4,128)S(1)} %get-tuple-element.89), channel_id=1, source_target_pairs={{8,0},{16,8},{24,16},{0,24},{9,1},{17,9},{25,17},{1,25},{10,2},{18... | collective-permute-start | bytes 122888 | tf_op jit(solution)/shard_map/ppermute | solution.py:20
  62.3 147.9 %collective-permute-start.3 = (f32[4,5,2,1,256]{4,0,3,2,1:T(4,128)S(1)}, f32[4,5,2,1,256]{4,0,3,2,1:T(4,128)S(1)}, u32[]{:S(2)}, u32[]{:S(2)}) collective-permute-start(f32[4,5,2,1,256]{4,0,3,2,1:T(4,128)S(1)} %get-tuple-element.88), channel_id=1, source_target_pairs={{0,8},{8,16},{16,24},{24,0},{1,9},{9,17},{17,25},{25,1},{2,10},{10... | collective-permute-start | bytes 122888 | tf_op jit(solution)/shard_map/ppermute | solution.py:19
  67.5 121.4 %copy-start.10 = (f32[2,256,256]{2,1,0:T(8,128)}, f32[2,256,256]{2,1,0:T(8,128)S(1)}, u32[]{:S(2)}) copy-start(f32[2,256,256]{2,1,0:T(8,128)S(1)} %get-tuple-element.74) | copy-start | bytes 1572868
  88.7 58.1 %copy-start.8 = (bf16[4,5,1,256,256]{4,0,3,2,1:T(4,128)(2,1)}, bf16[4,5,1,256,256]{4,0,3,2,1:T(4,128)(2,1)S(1)}, u32[]{:S(2)}) copy-start(bf16[4,5,1,256,256]{4,0,3,2,1:T(4,128)(2,1)S(1)} %collective-permute-done) | copy-start | bytes 7864324
  146.8 13.5 %copy-start.11 = (f32[2,256,256]{2,1,0:T(8,128)S(1)}, f32[2,256,256]{2,1,0:T(8,128)}, u32[]{:S(2)}) copy-start(f32[2,256,256]{2,1,0:T(8,128)} %get-tuple-element.75) | copy-start | bytes 1572868
  180.8 16.1 %slice-start = ((s8[5242880]{0:T(1024)(128)(4,1)}), s8[4194304]{0:T(1024)(128)(4,1)S(1)}, s32[]{:S(2)}) async-start(s8[5242880]{0:T(1024)(128)(4,1)} %bitcast.178), calls=%async_computation.2 | async-start | bytes 8388608
  254.8 21.0 %copy-start.22 = (f32[4,5,1024]{2,0,1:T(4,128)S(1)}, f32[4,5,1024]{2,0,1:T(4,128)}, u32[]{:S(2)}) copy-start(f32[4,5,1024]{2,0,1:T(4,128)} %param.13) | copy-start | bytes 245764
  261.8 59.0 %collective-permute-start.4 = (bf16[4,5,1,256,256]{4,0,3,2,1:T(4,128)(2,1)}, bf16[4,5,1,256,256]{4,0,3,2,1:T(4,128)(2,1)S(1)}, u32[]{:S(2)}, u32[]{:S(2)}) collective-permute-start(bf16[4,5,1,256,256]{4,0,3,2,1:T(4,128)(2,1)} %get-tuple-element.92), channel_id=1, source_target_pairs={{0,2},{2,4},{4,6},{1,3},{3,5},{5,7},{8,10},{10,12},{12,14},{9,11},... | collective-permute-start | bytes 7864328 | tf_op jit(solution)/shard_map/ppermute | solution.py:19
  265.3 112.4 %collective-permute-start.5 = (bf16[4,5,1,256,256]{4,0,3,2,1:T(4,128)(2,1)}, bf16[4,5,1,256,256]{4,0,3,2,1:T(4,128)(2,1)}, u32[]{:S(2)}, u32[]{:S(2)}) collective-permute-start(bf16[4,5,1,256,256]{4,0,3,2,1:T(4,128)(2,1)} %get-tuple-element.93), channel_id=1, source_target_pairs={{2,0},{4,2},{6,4},{3,1},{5,3},{7,5},{10,8},{12,10},{14,12},{11,9},... | collective-permute-start | bytes 7864328 | tf_op jit(solution)/shard_map/ppermute | solution.py:20
  270.2 8.3 %collective-permute-start.6 = (f32[4,5,2,1,256]{4,0,3,2,1:T(4,128)S(1)}, f32[4,5,2,1,256]{4,0,3,2,1:T(4,128)S(1)}, u32[]{:S(2)}, u32[]{:S(2)}) collective-permute-start(f32[4,5,2,1,256]{4,0,3,2,1:T(4,128)S(1)} %get-tuple-element.87), channel_id=1, source_target_pairs={{8,0},{16,8},{24,16},{0,24},{9,1},{17,9},{25,17},{1,25},{10,2},{18... | collective-permute-start | bytes 122888 | tf_op jit(solution)/shard_map/ppermute | solution.py:20
  278.4 164.9 %collective-permute-start.7 = (f32[4,5,2,1,256]{4,0,3,2,1:T(4,128)}, f32[4,5,2,1,256]{4,0,3,2,1:T(4,128)}, u32[]{:S(2)}, u32[]{:S(2)}) collective-permute-start(f32[4,5,2,1,256]{4,0,3,2,1:T(4,128)} %get-tuple-element.86), channel_id=1, source_target_pairs={{0,8},{8,16},{16,24},{24,0},{1,9},{9,17},{17,25},{25,1},{2,10},{10... | collective-permute-start | bytes 122888 | tf_op jit(solution)/shard_map/ppermute | solution.py:19
  395.8 15.5 %copy-start.1 = (f32[4,1,2,256,256]{4,0,3,2,1:T(4,128)}, f32[4,1,2,256,256]{4,0,3,2,1:T(4,128)S(1)}, u32[]{:S(2)}) copy-start(f32[4,1,2,256,256]{4,0,3,2,1:T(4,128)S(1)} %get-tuple-element.19) | copy-start | bytes 6291460
  395.8 15.5 %copy-start.2 = (f32[4,1,2,256,256]{4,0,3,2,1:T(4,128)}, f32[4,1,2,256,256]{4,0,3,2,1:T(4,128)S(1)}, u32[]{:S(2)}) copy-start(f32[4,1,2,256,256]{4,0,3,2,1:T(4,128)S(1)} %get-tuple-element.20) | copy-start | bytes 6291460
  395.8 15.5 %copy-start.3 = (f32[4,1,2,256,256]{4,0,3,2,1:T(4,128)}, f32[4,1,2,256,256]{4,0,3,2,1:T(4,128)S(1)}, u32[]{:S(2)}) copy-start(f32[4,1,2,256,256]{4,0,3,2,1:T(4,128)S(1)} %get-tuple-element.21) | copy-start | bytes 6291460
  395.8 15.5 %copy-start.4 = (f32[4,1,2,256,256]{4,0,3,2,1:T(4,128)}, f32[4,1,2,256,256]{4,0,3,2,1:T(4,128)S(1)}, u32[]{:S(2)}) copy-start(f32[4,1,2,256,256]{4,0,3,2,1:T(4,128)S(1)} %get-tuple-element.22) | copy-start | bytes 6291460
  418.4 25.0 %slice-start.2 = ((s8[10485760]{0:T(1024)(128)(4,1)}), s8[4194304]{0:T(1024)(128)(4,1)S(1)}, s32[]{:S(2)}) async-start(s8[10485760]{0:T(1024)(128)(4,1)} %bitcast.180), calls=%async_computation.4 | async-start | bytes 8388608
  418.4 25.0 %slice-start.3 = ((s8[10485760]{0:T(1024)(128)(4,1)}), s8[4194304]{0:T(1024)(128)(4,1)S(1)}, s32[]{:S(2)}) async-start(s8[10485760]{0:T(1024)(128)(4,1)} %bitcast.180), calls=%async_computation.5 | async-start | bytes 8388608
  428.1 15.3 %slice-start.4 = ((s8[10485760]{0:T(1024)(128)(4,1)}), s8[2097152]{0:T(1024)(128)(4,1)S(1)}, s32[]{:S(2)}) async-start(s8[10485760]{0:T(1024)(128)(4,1)} %bitcast.180), calls=%async_computation.6 | async-start | bytes 4194304
  428.1 15.3 %copy-start.16 = (f32[2,256,256]{2,1,0:T(8,128)S(1)}, f32[2,256,256]{2,1,0:T(8,128)}, u32[]{:S(2)}) copy-start(f32[2,256,256]{2,1,0:T(8,128)} %param.10) | copy-start | bytes 1572868
  428.1 15.3 %copy-start.19 = (f32[2,256,256]{2,1,0:T(8,128)S(1)}, f32[2,256,256]{2,1,0:T(8,128)}, u32[]{:S(2)}) copy-start(f32[2,256,256]{2,1,0:T(8,128)} %param.11) | copy-start | bytes 1572868
  428.1 15.3 %copy-start.21 = (f32[2,256,256]{2,1,0:T(8,128)S(1)}, f32[2,256,256]{2,1,0:T(8,128)}, u32[]{:S(2)}) copy-start(f32[2,256,256]{2,1,0:T(8,128)} %add_divide_fusion) | copy-start | bytes 1572868
  485.3 20.8 %copy-start.29 = (pred[1024]{0:T(1024)(128)(4,1)S(1)}, pred[1024]{0:T(1024)(128)(4,1)}, u32[]{:S(2)}) copy-start(pred[1024]{0:T(1024)(128)(4,1)} %compare_and_fusion) | copy-start | bytes 3076
  (17 other events, 153.6 us)
Sparse Core Ops, SparseCore 0:
  37.1 26.3 all-gather.1
  517.4 54.2 all-reduce.1
where the time goes:
time: 589 us; the launch traced here: 580 us
  waiting for transfers between devices  213 us (36%)
  other arithmetic  184 us (31%)
  local copies, waits for them, and re-layouts  105 us (18%)
  matrix products  45.8 us (8%)
  starting transfers between devices  18.7 us (3%)
  between operations  14.8 us (3%)
    ppermute x4, waiting for transfers between devices, with_halo(): after = lax.ppermute(leading, axis, down)  114 us
    unnamed x12, other arithmetic  92.5 us
    ppermute x4, waiting for transfers between devices, with_halo(): before = lax.ppermute(last, axis, up)  55 us
    unnamed x83, local copies, waits for them, and re-layouts  50.6 us
    dot_general x1, matrix products, body(): jnp.einsum('ab,avipk->bvipk', own_columns, lax.all_gather(start_rounded,...  44.5 us
    psum x1, waiting for transfers between devices, body(): diameter_modes = lax.psum(mode_terms, ('passage', 'tm'))  44.4 us
    convert_element_type x2, other arithmetic, neighbours(): with_halo(field.astype(jnp.bfloat16), (('cell', 2),), 1, False)  28.4 us
    add x1, other arithmetic, body(): field = field + (adjoint_source - applied - spectral_term) * scaling  28.2 us
  transfers between devices with their start and end apart: 10, of which 5 were waited for; matrix products, arithmetic and copies ran while one was open for 31% of the time, Pallas kernels for 0%

commit v1 on v0

--- a/solution.py
+++ b/solution.py
@@ -122,7 +122,7 @@
     )
     table = blade_table(PASSAGES)
     mode_terms = jnp.einsum("cmp,ps->cms", table, partial_sens, precision=lax.Precision.HIGHEST)
-    diameter_modes = lax.psum(mode_terms, ("passage", "tm"))
+    diameter_modes = jnp.sum(lax.all_gather(mode_terms, ("passage", "tm")), axis=0)
     return (field, diameter_modes)
 
 

time: 589 us -> 557 us (0.946)
  waiting for transfers between devices: 213 us -> 180 us
    psum x1 -> x0, waiting for transfers between devices: 44.4 us -> none  [body(): diameter_modes = lax.psum(mode_terms, ('passage', 'tm'))]
    all_gather x0 -> x1, waiting for transfers between devices: none -> 11.6 us  [body(): lax.all_gather(mode_terms, ('passage', 'tm'))]
    unnamed x83 -> x82, local copies, waits for them, and re-layouts: 50.6 us -> 49 us
  transfers between devices with their start and end apart: 10 -> 10, of which waited for: 5 -> 5; matrix products, arithmetic and copies ran while one was open for 31% -> 33% of each run, Pallas kernels for 0% -> 0%
where the time goes in v1:
time: 557 us; the launch traced here: 548 us
  other arithmetic  185 us (33%)
  waiting for transfers between devices  180 us (32%)
  local copies, waits for them, and re-layouts  103 us (18%)
  matrix products  45.8 us (8%)
  starting transfers between devices  18.7 us (3%)
  between operations  14.8 us (3%)
    ppermute x4, waiting for transfers between devices, with_halo(): after = lax.ppermute(leading, axis, down)  114 us
    unnamed x12, other arithmetic  92.5 us
    ppermute x4, waiting for transfers between devices, with_halo(): before = lax.ppermute(last, axis, up)  55 us
    unnamed x82, local copies, waits for them, and re-layouts  49 us
    dot_general x1, matrix products, body(): jnp.einsum('ab,avipk->bvipk', own_columns, lax.all_gather(start_rounded,...  44.5 us
    convert_element_type x2, other arithmetic, neighbours(): with_halo(field.astype(jnp.bfloat16), (('cell', 2),), 1, False)  28.4 us
    add x1, other arithmetic, body(): field = field + (adjoint_source - applied - spectral_term) * scaling  28.2 us
    gather x1, local copies, waits for them, and re-layouts, body(): picked = jnp.take(rows, surface_cells[0], axis=3)  20.8 us
  transfers between devices with their start and end apart: 10, of which 5 were waited for; matrix products, arithmetic and copies ran while one was open for 33% of the time, Pallas kernels for 0%

profile of v1, /device:TPU:0, one launch (start us, length us, event | category | flops | bytes accessed | tf_op | source)
XLA Modules:
  0.0 548.0 jit_solution(1463579063515243113)
XLA Ops:
  7.2 13.1 %copy.108 = bf16[4,5,2,256,256]{4,0,3,2,1:T(4,128)(2,1)} copy(f32[4,5,2,256,256]{4,3,2,1,0:T(8,128)} %param.7) | data formatting | bytes 15728640 | tf_op args[0]
  20.3 7.0 %fusion.71 = (bf16[4,5,1,256,256]{4,0,3,2,1:T(4,128)(2,1)}, bf16[4,5,1,256,256]{4,0,3,2,1:T(4,128)(2,1)}) fusion(bf16[4,5,2,256,256]{4,0,3,2,1:T(4,128)(2,1)} %copy.108), kind=kLoop, calls=%fused_computation.188 | loop fusion | bytes 10485760 | tf_op jit(solution)/shard_map/slice | solution.py:17
  27.4 5.0 collective-permute-start
  37.2 15.7 %constant_dynamic-update-slice_fusion.1 = (f32[4,5,2,257,256]{4,0,3,2,1:T(4,128)}, f32[4,5,2,256,256]{4,0,3,2,1:T(4,128)S(1)}) fusion(f32[4,5,2,256,256]{4,3,2,1,0:T(8,128)} %param.7), kind=kLoop, calls=%fused_computation.132 | loop fusion | bytes 31457280
  52.9 5.7 %copy-done.7 = f32[4,5,2,256,256]{4,0,3,2,1:T(4,128)} copy-done((f32[4,5,2,256,256]{4,0,3,2,1:T(4,128)}, f32[4,5,2,256,256]{4,0,3,2,1:T(4,128)S(1)}, u32[]{:S(2)}) %copy-start.7) | copy-done | bytes 10485784
  63.2 4.3 bitcast_convert_fusion
  71.4 3.9 bitcast_convert_fusion.9
  76.0 12.7 %collective-permute-done = bf16[4,5,1,256,256]{4,0,3,2,1:T(4,128)(2,1)S(1)} collective-permute-done((bf16[4,5,1,256,256]{4,0,3,2,1:T(4,128)(2,1)}, bf16[4,5,1,256,256]{4,0,3,2,1:T(4,128)(2,1)S(1)}, u32[]{:S(2)}, u32[]{:S(2)}) %collective-permute-start) | collective-permute-done | bytes 2621472 | tf_op jit(solution)/shard_map/ppermute | solution.py:19
  88.7 58.1 %collective-permute-done.1 = bf16[4,5,1,256,256]{4,0,3,2,1:T(4,128)(2,1)} collective-permute-done((bf16[4,5,1,256,256]{4,0,3,2,1:T(4,128)(2,1)}, bf16[4,5,1,256,256]{4,0,3,2,1:T(4,128)(2,1)}, u32[]{:S(2)}, u32[]{:S(2)}) %collective-permute-start.1) | collective-permute-done | bytes 2621472 | tf_op jit(solution)/shard_map/ppermute | solution.py:20
  146.8 13.4 %add_dynamic-update-slice_fusion.9 = (f32[4,5,2,256,256]{4,0,3,2,1:T(4,128)}, f32[4,1,2,256,256]{4,0,3,2,1:T(4,128)S(1)}, f32[4,1,2,256,256]{4,0,3,2,1:T(4,128)S...) fusion(f32[2,256,256]{2,1,0:T(8,128)} %get-tuple-element.76, ...), kind=kLoop, calls=%fused_computation.74 | loop fusion | flops 30932992 | bytes 59768832
  160.3 11.0 %add_dynamic-update-slice_fusion.8 = f32[4,5,2,256,256]{4,0,3,2,1:T(4,128)} fusion(f32[4,5,2,256,256]{4,0,3,2,1:T(4,128)} %get-tuple-element.25, f32[4,1,2,256,256]{4,0,3,2,1:T(4,128)} %get-tuple-element.35, f32[4,1,2,256,256]{4,0,3,2,1:T(4,128)S(1)} %get-tuple-element.34, f32[4,1,2,256,256]{4,0,3,2,1:T(4,128)S(1)} %get-tuple-element.33, ...), kind=kLoop, calls=%fused_computation.73 | loop fusion | flops 9961472 | bytes 28311552
  171.3 9.5 %add_dynamic-update-slice_fusion.7 = f32[4,5,2,256,256]{4,0,3,2,1:T(4,128)} fusion(f32[4,5,2,256,256]{4,0,3,2,1:T(4,128)} %add_dynamic-update-slice_fusion.8, f32[4,1,2,256,256]{4,0,3,2,1:T(4,128)} %get-tuple-element.35, f32[4,1,2,256,256]{4,0,3,2,1:T(4,128)S(1)} %get-tuple-element.34, f32[4,1,2,256,256]{4,0,3,2,1:T(4,128)S(1)} %get-tuple-element.33, ...), kind=kLoop, calls=%fused_computation.72 | loop fusion | flops 9961472 | bytes 28311552
  180.8 8.1 %add_dynamic-update-slice_fusion.6 = f32[4,5,2,256,256]{4,0,3,2,1:T(4,128)} fusion(f32[4,5,2,256,256]{4,0,3,2,1:T(4,128)} %add_dynamic-update-slice_fusion.7, f32[4,1,2,256,256]{4,0,3,2,1:T(4,128)} %get-tuple-element.35, f32[4,1,2,256,256]{4,0,3,2,1:T(4,128)} %copy-done.6, f32[4,1,2,256,256]{4,0,3,2,1:T(4,128)} %copy-done.5, ...), kind=kLoop, calls=%fused_computation.71 | loop fusion | flops 9961472 | bytes 28311552
  188.9 8.0 %add_dynamic-update-slice_fusion.5 = f32[4,5,2,256,256]{4,0,3,2,1:T(4,128)} fusion(f32[4,5,2,256,256]{4,0,3,2,1:T(4,128)} %add_dynamic-update-slice_fusion.6, f32[4,1,2,256,256]{4,0,3,2,1:T(4,128)} %get-tuple-element.35, f32[4,1,2,256,256]{4,0,3,2,1:T(4,128)} %copy-done.6, f32[4,1,2,256,256]{4,0,3,2,1:T(4,128)} %copy-done.5, ...), kind=kLoop, calls=%fused_computation.70 | loop fusion | flops 9961472 | bytes 28311552 | tf_op jit(solution)/shard_map/stack | solution.py:57
  197.0 13.2 %maximum_convert_fusion = f32[4,5,4,256,256]{4,0,3,2,1:T(4,128)} fusion(bf16[4,5,1,256,256]{4,0,3,2,1:T(4,128)(2,1)} %collective-permute-done.1, bf16[4,5,2,256,256]{4,0,3,2,1:T(4,128)(2,1)S(1)} %bitcast.180, bf16[4,5,1,256,256]{4,0,3,2,1:T(4,128)(2,1)} %copy-done.8), kind=kLoop, calls=%fused_computation.30 | loop fusion | flops 15728640 | bytes 31457280 | tf_op jit(solution)/shard_map/convert_element_type | solution.py:64
  210.2 44.5 %fusion.66 = (bf16[4,5,2,256,256]{4,0,3,2,1:T(4,128)(2,1)}, f32[4,5,2,256,256]{4,0,3,2,1:T(4,128)}, f32[4,5,2,256,256]{4,0,3,2,1:T(4,128)}) fusion(f32[4,5,2,256,256]{4,0,3,2,1:T(4,128)} %copy-done.7, f32[2,256,256]{2,1,0:T(8,128)S(1)} %copy-done.20, f32[4,5,2,256,256]{4,0,3,2,1:T(4,128)} %add_dynamic-update-slice_fusion.5, ...), kind=kOutput, calls=%fused_computation.184 | convolution fusion | flops 290979840 | bytes 101230592 | tf_op jit(solution)/shard_map/ab,avipk->bvipk/dot_general | solution.py:87
  254.8 7.0 %fusion.70 = (bf16[4,5,1,256,256]{4,0,3,2,1:T(4,128)(2,1)}, bf16[4,5,1,256,256]{4,0,3,2,1:T(4,128)(2,1)}) fusion(bf16[4,5,2,256,256]{4,0,3,2,1:T(4,128)(2,1)} %get-tuple-element.23), kind=kLoop, calls=%fused_computation.187 | loop fusion | bytes 10485760 | tf_op jit(solution)/shard_map/slice | solution.py:17
  278.4 42.3 %collective-permute-done.4 = bf16[4,5,1,256,256]{4,0,3,2,1:T(4,128)(2,1)S(1)} collective-permute-done((bf16[4,5,1,256,256]{4,0,3,2,1:T(4,128)(2,1)}, bf16[4,5,1,256,256]{4,0,3,2,1:T(4,128)(2,1)S(1)}, u32[]{:S(2)}, u32[]{:S(2)}) %collective-permute-start.4) | collective-permute-done | bytes 2621472 | tf_op jit(solution)/shard_map/ppermute | solution.py:19
  322.3 55.4 %collective-permute-done.5 = bf16[4,5,1,256,256]{4,0,3,2,1:T(4,128)(2,1)} collective-permute-done((bf16[4,5,1,256,256]{4,0,3,2,1:T(4,128)(2,1)}, bf16[4,5,1,256,256]{4,0,3,2,1:T(4,128)(2,1)}, u32[]{:S(2)}, u32[]{:S(2)}) %collective-permute-start.5) | collective-permute-done | bytes 2621472 | tf_op jit(solution)/shard_map/ppermute | solution.py:20
  377.7 18.1 %add_dynamic-update-slice_fusion.4 = (f32[4,5,2,256,256]{4,0,3,2,1:T(4,128)}, f32[4,1,2,256,256]{4,0,3,2,1:T(4,128)S(1)}, f32[4,1,2,256,256]{4,0,3,2,1:T(4,128)S...) fusion(f32[2,256,256]{2,1,0:T(8,128)} %get-tuple-element.76, ...), kind=kLoop, calls=%fused_computation.69 | loop fusion | flops 33554432 | bytes 59809792
  395.8 8.4 %add_dynamic-update-slice_fusion.3 = f32[4,5,2,256,256]{4,0,3,2,1:T(4,128)} fusion(f32[4,5,2,256,256]{4,0,3,2,1:T(4,128)} %get-tuple-element.12, f32[4,1,2,256,256]{4,0,3,2,1:T(4,128)S(1)} %get-tuple-element.22, f32[4,1,2,256,256]{4,0,3,2,1:T(4,128)S(1)} %get-tuple-element.21, f32[4,1,2,256,256]{4,0,3,2,1:T(4,128)S(1)} %get-tuple-element.20, ...), kind=kLoop, calls=%fused_computation.68 | loop fusion | flops 9961472 | bytes 28311552
  404.2 7.0 %add_dynamic-update-slice_fusion.2 = f32[4,5,2,256,256]{4,0,3,2,1:T(4,128)} fusion(f32[4,5,2,256,256]{4,0,3,2,1:T(4,128)} %add_dynamic-update-slice_fusion.3, f32[4,1,2,256,256]{4,0,3,2,1:T(4,128)S(1)} %get-tuple-element.22, f32[4,1,2,256,256]{4,0,3,2,1:T(4,128)S(1)} %get-tuple-element.21, f32[4,1,2,256,256]{4,0,3,2,1:T(4,128)S(1)} %get-tuple-element.20, ...), kind=kLoop, calls=%fused_computation.67 | loop fusion | flops 9961472 | bytes 28311552
  411.3 7.1 %add_dynamic-update-slice_fusion.1 = f32[4,5,2,256,256]{4,0,3,2,1:T(4,128)} fusion(f32[4,5,2,256,256]{4,0,3,2,1:T(4,128)} %add_dynamic-update-slice_fusion.2, f32[4,1,2,256,256]{4,0,3,2,1:T(4,128)S(1)} %get-tuple-element.22, f32[4,1,2,256,256]{4,0,3,2,1:T(4,128)S(1)} %get-tuple-element.21, f32[4,1,2,256,256]{4,0,3,2,1:T(4,128)S(1)} %get-tuple-element.20, ...), kind=kLoop, calls=%fused_computation.66 | loop fusion | flops 9961472 | bytes 28311552
  418.4 9.7 %add_dynamic-update-slice_fusion = f32[4,5,2,256,256]{4,0,3,2,1:T(4,128)} fusion(f32[4,5,2,256,256]{4,0,3,2,1:T(4,128)} %add_dynamic-update-slice_fusion.1, f32[4,1,2,256,256]{4,0,3,2,1:T(4,128)} %copy-done.4, f32[4,1,2,256,256]{4,0,3,2,1:T(4,128)} %copy-done.3, f32[4,1,2,256,256]{4,0,3,2,1:T(4,128)} %copy-done.2, f32[4,1,2,256,256]{4,0,3,2,1:T(4,128)} %copy-done.1, ...), kind=kLoop, calls=%fused_computation.65 | loop fusion | flops 9961472 | bytes 28311552 | tf_op jit(solution)/shard_map/stack | solution.py:57
  428.2 15.2 %maximum_convert_fusion.1 = f32[4,5,4,256,256]{4,0,3,2,1:T(4,128)} fusion(bf16[4,5,1,256,256]{4,0,3,2,1:T(4,128)(2,1)} %collective-permute-done.5, bf16[4,5,2,256,256]{4,0,3,2,1:T(4,128)(2,1)} %get-tuple-element.23, bf16[4,5,1,256,256]{4,0,3,2,1:T(4,128)(2,1)} %copy-done.9), kind=kLoop, calls=%fused_computation.31 | loop fusion | flops 15728640 | bytes 31457280 | tf_op jit(solution)/shard_map/convert_element_type | solution.py:64
  443.4 28.2 %multiply_add_fusion = f32[4,5,2,256,256]{4,0,3,2,1:T(4,128)} fusion(f32[4,5,2,256,256]{4,0,3,2,1:T(4,128)S(1)} %bitcast.182, f32[4,5,2,256,256]{4,0,3,2,1:T(4,128)} %get-tuple-element.97, f32[4,5,2,256,256]{4,0,3,2,1:T(4,128)} %add_dynamic-update-slice_fusion, f32[4,5,2,1,256]{4,0,3,2,1:T(4,128)} %collective-permute-done.7, ...), kind=kLoop, calls=%fused_computation.35 | loop fusion | flops 39321600 | bytes 75055104 | tf_op jit(solution)/shard_map/add | solution.py:100
  471.7 5.5 %gather_fusion = f32[32,4,5,2,256]{4,1,3,2,0:T(4,128)S(1)} fusion(f32[4,5,2,256,256]{4,0,3,2,1:T(4,128)} %multiply_add_fusion, s32[1024]{0:T(1024)} %pad_clamp_fusion), kind=kCustom, calls=%fused_computation | custom fusion | bytes 2621568 | tf_op jit(solution)/shard_map/jit(_take)/gather | solution.py:113
  478.3 7.1 %copy.94 = f32[4,5,16,2,2,256]{2,0,5,4,3,1:T(4,128)} copy(f32[4,5,16,2,2,256]{5,4,3,2,1,0:T(2,128)S(1)} %fusion.28) | data formatting | bytes 2621440 | tf_op jit(solution)/shard_map/reshape | solution.py:116
  485.3 20.8 %gather_fusion.1 = f32[1024,4,5,16]{3,1,2,0:T(4,128)} fusion(f32[4,5,16,1024]{2,0,3,1:T(4,128)} %bitcast.183, s32[1024]{0:T(1024)S(1)} %copy-done.25), kind=kCustom, calls=%fused_computation.1 | custom fusion | bytes 2625536 | tf_op jit(solution)/shard_map/jit(_take)/gather | solution.py:119
  506.1 9.9 %multiply_reduce_fusion = f32[1024,16]{1,0:T(8,128)S(1)} fusion(f32[1024,4,5,16]{3,1,2,0:T(4,128)} %gather_fusion.1, f32[1024,4,5]{1,2,0:T(8,128)} %copy.96, pred[1024]{0:T(1024)(128)(4,1)S(1)} %copy-done.29), kind=kLoop, calls=%fused_computation.32 | loop fusion | flops 966656 | bytes 1459200
  517.3 10.1 %copy.85 = f32[4,5,2,256,256]{4,3,2,1,0:T(8,128)} copy(f32[4,5,2,256,256]{4,0,3,2,1:T(4,128)} %multiply_add_fusion) | data formatting | bytes 20971520
  527.4 11.6 %all-gather.6.cloned.1.call-done = f32[16,16,1024]{2,1,0:T(8,128)} async-done(((f32[2,16,1024]{2,1,0:T(8,128)}), f32[16,16,1024]{2,1,0:T(8,128)}) %all-gather.6.cloned.1.call-update) | async-done | bytes 1048592 | tf_op jit(solution)/shard_map/all_gather | solution.py:125
  (120 shorter events, 36.5 us)
Async XLA Ops:
  7.2 203.1 %all-gather.4.cloned.1.call-start = ((), (), s32[]{:S(2)}) async-start(), calls=%async_computation | async-start | bytes 15728640 | tf_op jit(solution)/shard_map/all_gather | solution.py:90
  20.3 13.4 %copy-start = (bf16[4,5,2,256,256]{4,0,3,2,1:T(4,128)(2,1)S(1)}, bf16[4,5,2,256,256]{4,0,3,2,1:T(4,128)(2,1)}, u32[]{:S(2)}) copy-start(bf16[4,5,2,256,256]{4,0,3,2,1:T(4,128)(2,1)} %copy.108) | copy-start | bytes 15728644
  27.4 61.3 %collective-permute-start = (bf16[4,5,1,256,256]{4,0,3,2,1:T(4,128)(2,1)}, bf16[4,5,1,256,256]{4,0,3,2,1:T(4,128)(2,1)S(1)}, u32[]{:S(2)}, u32[]{:S(2)}) collective-permute-start(bf16[4,5,1,256,256]{4,0,3,2,1:T(4,128)(2,1)} %get-tuple-element.94), channel_id=1, source_target_pairs={{0,2},{2,4},{4,6},{1,3},{3,5},{5,7},{8,10},{10,12},{12,14},{9,11},... | collective-permute-start | bytes 7864328 | tf_op jit(solution)/shard_map/ppermute | solution.py:19
  32.4 114.4 %collective-permute-start.1 = (bf16[4,5,1,256,256]{4,0,3,2,1:T(4,128)(2,1)}, bf16[4,5,1,256,256]{4,0,3,2,1:T(4,128)(2,1)}, u32[]{:S(2)}, u32[]{:S(2)}) collective-permute-start(bf16[4,5,1,256,256]{4,0,3,2,1:T(4,128)(2,1)} %get-tuple-element.95), channel_id=1, source_target_pairs={{2,0},{4,2},{6,4},{3,1},{5,3},{7,5},{10,8},{12,10},{14,12},{11,9},... | collective-permute-start | bytes 7864328 | tf_op jit(solution)/shard_map/ppermute | solution.py:20
  37.0 25.3 %copy-start.14 = (f32[2,256,256]{2,1,0:T(8,128)S(1)}, f32[2,256,256]{2,1,0:T(8,128)}, u32[]{:S(2)}) copy-start(f32[2,256,256]{2,1,0:T(8,128)} %param.10) | copy-start | bytes 1572868
  37.0 502.1 %all-gather.6.cloned.1.call-start = ((), (), s32[]{:S(2)}) async-start(), calls=%async_computation.1 | async-start | bytes 1179648 | tf_op jit(solution)/shard_map/all_gather | solution.py:125
  37.2 25.1 %copy-start.17 = (f32[2,256,256]{2,1,0:T(8,128)S(1)}, f32[2,256,256]{2,1,0:T(8,128)}, u32[]{:S(2)}) copy-start(f32[2,256,256]{2,1,0:T(8,128)} %param.11) | copy-start | bytes 1572868
  37.2 30.3 %slice-start.5 = ((s8[13107200]{0:T(1024)(128)(4,1)}), s8[4194304]{0:T(1024)(128)(4,1)S(1)}, s32[]{:S(2)}) async-start(s8[13107200]{0:T(1024)(128)(4,1)} %bitcast.184), calls=%async_computation.7 | async-start | bytes 8388608
  37.2 30.3 %slice-start.6 = ((s8[13107200]{0:T(1024)(128)(4,1)}), s8[4194304]{0:T(1024)(128)(4,1)S(1)}, s32[]{:S(2)}) async-start(s8[13107200]{0:T(1024)(128)(4,1)} %bitcast.184), calls=%async_computation.8 | async-start | bytes 8388608
  37.2 30.3 %slice-start.7 = ((s8[13107200]{0:T(1024)(128)(4,1)}), s8[4194304]{0:T(1024)(128)(4,1)S(1)}, s32[]{:S(2)}) async-start(s8[13107200]{0:T(1024)(128)(4,1)} %bitcast.184), calls=%async_computation.9 | async-start | bytes 8388608
  58.6 16.7 %collective-permute-start.2 = (f32[4,5,2,1,256]{4,0,3,2,1:T(4,128)S(1)}, f32[4,5,2,1,256]{4,0,3,2,1:T(4,128)S(1)}, u32[]{:S(2)}, u32[]{:S(2)}) collective-permute-start(f32[4,5,2,1,256]{4,0,3,2,1:T(4,128)S(1)} %get-tuple-element.89), channel_id=1, source_target_pairs={{8,0},{16,8},{24,16},{0,24},{9,1},{17,9},{25,17},{1,25},{10,2},{18... | collective-permute-start | bytes 122888 | tf_op jit(solution)/shard_map/ppermute | solution.py:20
  62.3 147.9 %collective-permute-start.3 = (f32[4,5,2,1,256]{4,0,3,2,1:T(4,128)S(1)}, f32[4,5,2,1,256]{4,0,3,2,1:T(4,128)S(1)}, u32[]{:S(2)}, u32[]{:S(2)}) collective-permute-start(f32[4,5,2,1,256]{4,0,3,2,1:T(4,128)S(1)} %get-tuple-element.88), channel_id=1, source_target_pairs={{0,8},{8,16},{16,24},{24,0},{1,9},{9,17},{17,25},{25,1},{2,10},{10... | collective-permute-start | bytes 122888 | tf_op jit(solution)/shard_map/ppermute | solution.py:19
  67.5 121.4 %copy-start.10 = (f32[2,256,256]{2,1,0:T(8,128)}, f32[2,256,256]{2,1,0:T(8,128)S(1)}, u32[]{:S(2)}) copy-start(f32[2,256,256]{2,1,0:T(8,128)S(1)} %get-tuple-element.74) | copy-start | bytes 1572868
  88.7 58.1 %copy-start.8 = (bf16[4,5,1,256,256]{4,0,3,2,1:T(4,128)(2,1)}, bf16[4,5,1,256,256]{4,0,3,2,1:T(4,128)(2,1)S(1)}, u32[]{:S(2)}) copy-start(bf16[4,5,1,256,256]{4,0,3,2,1:T(4,128)(2,1)S(1)} %collective-permute-done) | copy-start | bytes 7864324
  146.8 13.5 %copy-start.11 = (f32[2,256,256]{2,1,0:T(8,128)S(1)}, f32[2,256,256]{2,1,0:T(8,128)}, u32[]{:S(2)}) copy-start(f32[2,256,256]{2,1,0:T(8,128)} %get-tuple-element.75) | copy-start | bytes 1572868
  180.8 16.1 %slice-start = ((s8[5242880]{0:T(1024)(128)(4,1)}), s8[4194304]{0:T(1024)(128)(4,1)S(1)}, s32[]{:S(2)}) async-start(s8[5242880]{0:T(1024)(128)(4,1)} %bitcast.179), calls=%async_computation.2 | async-start | bytes 8388608
  254.8 21.0 %copy-start.22 = (f32[4,5,1024]{2,0,1:T(4,128)S(1)}, f32[4,5,1024]{2,0,1:T(4,128)}, u32[]{:S(2)}) copy-start(f32[4,5,1024]{2,0,1:T(4,128)} %param.13) | copy-start | bytes 245764
  261.8 59.0 %collective-permute-start.4 = (bf16[4,5,1,256,256]{4,0,3,2,1:T(4,128)(2,1)}, bf16[4,5,1,256,256]{4,0,3,2,1:T(4,128)(2,1)S(1)}, u32[]{:S(2)}, u32[]{:S(2)}) collective-permute-start(bf16[4,5,1,256,256]{4,0,3,2,1:T(4,128)(2,1)} %get-tuple-element.92), channel_id=1, source_target_pairs={{0,2},{2,4},{4,6},{1,3},{3,5},{5,7},{8,10},{10,12},{12,14},{9,11},... | collective-permute-start | bytes 7864328 | tf_op jit(solution)/shard_map/ppermute | solution.py:19
  265.3 112.4 %collective-permute-start.5 = (bf16[4,5,1,256,256]{4,0,3,2,1:T(4,128)(2,1)}, bf16[4,5,1,256,256]{4,0,3,2,1:T(4,128)(2,1)}, u32[]{:S(2)}, u32[]{:S(2)}) collective-permute-start(bf16[4,5,1,256,256]{4,0,3,2,1:T(4,128)(2,1)} %get-tuple-element.93), channel_id=1, source_target_pairs={{2,0},{4,2},{6,4},{3,1},{5,3},{7,5},{10,8},{12,10},{14,12},{11,9},... | collective-permute-start | bytes 7864328 | tf_op jit(solution)/shard_map/ppermute | solution.py:20
  270.2 8.3 %collective-permute-start.6 = (f32[4,5,2,1,256]{4,0,3,2,1:T(4,128)S(1)}, f32[4,5,2,1,256]{4,0,3,2,1:T(4,128)S(1)}, u32[]{:S(2)}, u32[]{:S(2)}) collective-permute-start(f32[4,5,2,1,256]{4,0,3,2,1:T(4,128)S(1)} %get-tuple-element.87), channel_id=1, source_target_pairs={{8,0},{16,8},{24,16},{0,24},{9,1},{17,9},{25,17},{1,25},{10,2},{18... | collective-permute-start | bytes 122888 | tf_op jit(solution)/shard_map/ppermute | solution.py:20
  278.4 164.9 %collective-permute-start.7 = (f32[4,5,2,1,256]{4,0,3,2,1:T(4,128)}, f32[4,5,2,1,256]{4,0,3,2,1:T(4,128)}, u32[]{:S(2)}, u32[]{:S(2)}) collective-permute-start(f32[4,5,2,1,256]{4,0,3,2,1:T(4,128)} %get-tuple-element.86), channel_id=1, source_target_pairs={{0,8},{8,16},{16,24},{24,0},{1,9},{9,17},{17,25},{25,1},{2,10},{10... | collective-permute-start | bytes 122888 | tf_op jit(solution)/shard_map/ppermute | solution.py:19
  395.8 15.5 %copy-start.1 = (f32[4,1,2,256,256]{4,0,3,2,1:T(4,128)}, f32[4,1,2,256,256]{4,0,3,2,1:T(4,128)S(1)}, u32[]{:S(2)}) copy-start(f32[4,1,2,256,256]{4,0,3,2,1:T(4,128)S(1)} %get-tuple-element.19) | copy-start | bytes 6291460
  395.8 15.5 %copy-start.2 = (f32[4,1,2,256,256]{4,0,3,2,1:T(4,128)}, f32[4,1,2,256,256]{4,0,3,2,1:T(4,128)S(1)}, u32[]{:S(2)}) copy-start(f32[4,1,2,256,256]{4,0,3,2,1:T(4,128)S(1)} %get-tuple-element.20) | copy-start | bytes 6291460
  395.8 15.5 %copy-start.3 = (f32[4,1,2,256,256]{4,0,3,2,1:T(4,128)}, f32[4,1,2,256,256]{4,0,3,2,1:T(4,128)S(1)}, u32[]{:S(2)}) copy-start(f32[4,1,2,256,256]{4,0,3,2,1:T(4,128)S(1)} %get-tuple-element.21) | copy-start | bytes 6291460
  395.8 15.5 %copy-start.4 = (f32[4,1,2,256,256]{4,0,3,2,1:T(4,128)}, f32[4,1,2,256,256]{4,0,3,2,1:T(4,128)S(1)}, u32[]{:S(2)}) copy-start(f32[4,1,2,256,256]{4,0,3,2,1:T(4,128)S(1)} %get-tuple-element.22) | copy-start | bytes 6291460
  418.4 25.0 %slice-start.2 = ((s8[10485760]{0:T(1024)(128)(4,1)}), s8[4194304]{0:T(1024)(128)(4,1)S(1)}, s32[]{:S(2)}) async-start(s8[10485760]{0:T(1024)(128)(4,1)} %bitcast.181), calls=%async_computation.4 | async-start | bytes 8388608
  418.4 25.0 %slice-start.3 = ((s8[10485760]{0:T(1024)(128)(4,1)}), s8[4194304]{0:T(1024)(128)(4,1)S(1)}, s32[]{:S(2)}) async-start(s8[10485760]{0:T(1024)(128)(4,1)} %bitcast.181), calls=%async_computation.5 | async-start | bytes 8388608
  428.1 15.3 %slice-start.4 = ((s8[10485760]{0:T(1024)(128)(4,1)}), s8[2097152]{0:T(1024)(128)(4,1)S(1)}, s32[]{:S(2)}) async-start(s8[10485760]{0:T(1024)(128)(4,1)} %bitcast.181), calls=%async_computation.6 | async-start | bytes 4194304
  428.1 15.3 %copy-start.16 = (f32[2,256,256]{2,1,0:T(8,128)S(1)}, f32[2,256,256]{2,1,0:T(8,128)}, u32[]{:S(2)}) copy-start(f32[2,256,256]{2,1,0:T(8,128)} %param.10) | copy-start | bytes 1572868
  428.1 15.3 %copy-start.19 = (f32[2,256,256]{2,1,0:T(8,128)S(1)}, f32[2,256,256]{2,1,0:T(8,128)}, u32[]{:S(2)}) copy-start(f32[2,256,256]{2,1,0:T(8,128)} %param.11) | copy-start | bytes 1572868
  428.1 15.3 %copy-start.21 = (f32[2,256,256]{2,1,0:T(8,128)S(1)}, f32[2,256,256]{2,1,0:T(8,128)}, u32[]{:S(2)}) copy-start(f32[2,256,256]{2,1,0:T(8,128)} %add_divide_fusion) | copy-start | bytes 1572868
  485.3 20.8 %copy-start.29 = (pred[1024]{0:T(1024)(128)(4,1)S(1)}, pred[1024]{0:T(1024)(128)(4,1)}, u32[]{:S(2)}) copy-start(pred[1024]{0:T(1024)(128)(4,1)} %compare_and_fusion) | copy-start | bytes 3076
  (17 other events, 153.6 us)
Sparse Core Ops, SparseCore 0:
  37.1 26.3 all-gather.3
  517.4 21.5 all-gather.5
